TPU v7x, 128 devices: a whole 4x4x4 slice. The times are simulated.
128 devices in a mesh: req: 16 (over x, y), head: 8 (over z, core).
Axes of the slice: x: 4, y: 4, z: 4, core: 2. Of those that a mesh axis runs over, the one named last changes fastest.
Arguments:
- streams: bfloat16 [12288, 4, 2048], P('req', None, 'head'), may hold values from -6 to 6
- hc_in: float32 [2, 4], replicated, may hold values from 0.2 to 1
- hc_mix: float32 [2, 4, 4], replicated, may hold values from -0.4 to 0.4
- hc_out: float32 [2, 4], replicated, may hold values from 0.5 to 1.5
- qkv_weight: bfloat16 [2048, 3, 2048], P(None, None, 'head'), may hold values from -0.125 to 0.125
- out_weight: bfloat16 [2048, 2048], P('head'), may hold values from -0.125 to 0.125
- up_gate: bfloat16 [2048, 2, 8192], P(None, None, 'head'), may hold values from -0.125 to 0.125
- down_weight: bfloat16 [8192, 2048], P('head'), may hold values from -0.0625 to 0.0625
- draft_weight: bfloat16 [2, 2048, 2048], P(None, None, 'head'), may hold values from -0.125 to 0.125
- lm_head: bfloat16 [2048, 50304], P(None, ('req', 'head')), may hold values from -0.125 to 0.125
- k_pages: bfloat16 [768, 128, 16, 128], P('req', None, 'head'), may hold values from -45 to 45
- v_pages: bfloat16 [768, 128, 16, 128], P('req', None, 'head'), may hold values from -6 to 6
- page_owner: int32 [768], P('req'), may hold values from -1 to 255, as said below
- page_fill: int32 [768], P('req'), may hold values from 0 to 128, as said below
- cache_len: int32 [256], P('req'), may hold values from 1 to 16384, as said below
- tree_parent: int32 [256, 48], P('req'), may hold values from 0 to 46, as said below
- accepted_index: int32 [256], P('req'), may hold values from 0 to 47
Outputs:
- new_streams: bfloat16 [12288, 4, 2048], P('req', None, 'head')
- logits: float32 [256, 2, 50304], P(('req', 'head'))
Inputs may be any that keep to these rules, and one draw needn't show every extreme that they name: `page_owner`: each page slot holds one page of the request it names, or -1 where it is empty. Every request owns at least one page and one request owns 128 pages; the live pages of a device's slots vary widely from device to device. `page_fill`: 0 for an empty slot; every page of a request is full except at most one. `cache_len`: equals the valid entries of the pages the request owns; one request has exactly 16384. `tree_parent`: entry i names a smaller position, the parent of position i; position 0 is the root and names itself.
All inputs are finite; a program needn't handle non-finite values.
Results may differ from a plain program's by a relative error of at most 0.027.
Values may be sent and summed in bfloat16 or wider, within the bound.
A program may use at most 512 MiB of HBM per device.

v0:
```python
import math
import jax
import jax.numpy as jnp
from jax import lax
from jax.sharding import PartitionSpec as P

NEG_FILL = -1e30
PRECISE = lax.Precision.HIGHEST


def layer_norm(values):
    center = jnp.mean(values, axis=-1, keepdims=True)
    square = jnp.mean(values * values, axis=-1, keepdims=True)
    return (values - center) * lax.rsqrt(square - center * center + 1e-05)


def normalize(values, sums, squares, width):
    center = sums / width
    return (values - center) * lax.rsqrt(squares / width - center * center + 1e-05)


def ancestors(parents):
    length = parents.shape[1]
    places = jnp.arange(length, dtype=jnp.int32)
    linked = (parents[:, :, None] == places[None, None, :]) | (places[:, None] == places[None, :])[
        None
    ]
    reach = linked.astype(jnp.float32)
    for repeat in range(max(1, (length - 1).bit_length())):
        reach = jnp.minimum(jnp.einsum("jik,jkl->jil", reach, reach, precision=PRECISE), 1.0)
    return reach


def rotate(values, positions):
    half = values.shape[-1] // 2
    freqs = jnp.exp(
        jnp.arange(half, dtype=jnp.float32) * (-2.0 * math.log(10000.0) / values.shape[-1])
    )
    angles = positions.astype(jnp.float32)[:, None] * freqs[None, :]
    cosine = jnp.cos(angles)[:, None, :]
    sine = jnp.sin(angles)[:, None, :]
    first = values[..., :half]
    second = values[..., half:]
    return jnp.concatenate(
        [first * cosine - second * sine, second * cosine + first * sine], axis=-1
    )


def blend(stream_vals, weights):
    total = weights[0] * stream_vals[:, 0]
    for index in range(1, stream_vals.shape[1]):
        total = total + weights[index] * stream_vals[:, index]
    return total


def remix(stream_vals, mixing, out_scale, delta):
    count = stream_vals.shape[1]
    matrix = jnp.eye(count, dtype=jnp.float32) + mixing
    rows = [
        blend(stream_vals, matrix[:, target]) + out_scale[target] * delta for target in range(count)
    ]
    return jnp.stack(rows, axis=1)


def stream_total(stream_vals):
    total = stream_vals[:, 0]
    for index in range(1, stream_vals.shape[1]):
        total = total + stream_vals[:, index]
    return total


def fold_rows(weight, piece):
    return jnp.dot(piece, weight, preferred_element_type=jnp.float32)


def on_device(
    streams,
    hc_in,
    hc_mix,
    hc_out,
    qkv_weight,
    out_weight,
    up_gate,
    down_weight,
    draft_weight,
    lm_head,
    k_pages,
    v_pages,
    page_owner,
    page_fill,
    cache_len,
    tree_parent,
    accepted_index,
):
    tokens_local = streams.shape[0]
    feature_local = streams.shape[2]
    width = qkv_weight.shape[0]
    req_local = cache_len.shape[0]
    tree_size = tree_parent.shape[1]
    slot_count = k_pages.shape[0]
    page_size = k_pages.shape[1]
    heads_local = k_pages.shape[2]
    head_dim = k_pages.shape[3]
    draft_count = draft_weight.shape[0]
    all_requests = req_local * lax.axis_size("req")
    reach = ancestors(tree_parent)
    depth = (jnp.sum(reach, axis=2) - 1.0).astype(jnp.int32)
    positions = (cache_len[:, None] + depth).reshape(tokens_local)
    stream_vals = streams.astype(jnp.float32)
    mixed_in = blend(stream_vals, hc_in[0])
    stat_sum, stat_square = lax.psum(
        (jnp.sum(mixed_in, axis=1), jnp.sum(mixed_in * mixed_in, axis=1)), "head"
    )
    normed = normalize(mixed_in, stat_sum[:, None], stat_square[:, None], width).astype(
        jnp.bfloat16
    )
    qkv_flat = qkv_weight.reshape(width, -1)
    projected = fold_rows(qkv_flat, lax.all_gather(normed, "head", axis=1, tiled=True))
    projected = projected.reshape(tokens_local, 3, heads_local, head_dim)
    queries = (rotate(projected[:, 0], positions) * head_dim ** (-0.5)).astype(jnp.bfloat16)
    keys_new = rotate(projected[:, 1], positions).astype(jnp.bfloat16)
    values_new = projected[:, 2].astype(jnp.bfloat16)
    gathered = lax.all_gather(
        queries.reshape(req_local, tree_size, heads_local * head_dim), "req", axis=0, tiled=True
    )
    query_all = gathered.reshape(all_requests, tree_size, heads_local, head_dim)
    safe_owner = jnp.maximum(page_owner, 0)
    live = (page_owner >= 0)[:, None] & (
        jnp.arange(page_size, dtype=jnp.int32)[None, :] < page_fill[:, None]
    )
    cache_scores = jnp.einsum(
        "pqhd,pkhd->pqhk", query_all[safe_owner], k_pages, preferred_element_type=jnp.float32
    )
    cache_scores = jnp.where(live[:, None, None, :], cache_scores, NEG_FILL)
    page_top = jnp.max(cache_scores, axis=3)
    owned_mask = page_owner[:, None] == jnp.arange(all_requests, dtype=jnp.int32)[None, :]
    owned = owned_mask.astype(jnp.float32)
    local_top = jnp.max(
        jnp.where(owned_mask[:, :, None, None], page_top[:, None], NEG_FILL), axis=0
    )
    first_request = lax.axis_index("req") * req_local
    global_top = lax.pmax(local_top.astype(jnp.bfloat16), "req").astype(local_top.dtype)
    weights = jnp.where(
        live[:, None, None, :], jnp.exp(cache_scores - global_top[safe_owner][..., None]), 0.0
    )
    page_den = jnp.sum(weights, axis=3)
    page_num = jnp.einsum(
        "pqhk,pkhd->pqhd", weights.astype(jnp.bfloat16), v_pages, preferred_element_type=jnp.float32
    )
    summed = jnp.dot(owned.T, page_num.reshape(slot_count, -1), precision=PRECISE)
    totals = jnp.dot(owned.T, page_den.reshape(slot_count, -1), precision=PRECISE)
    summed, totals = (
        summed.reshape(all_requests, tree_size, heads_local, head_dim),
        totals.reshape(all_requests, tree_size, heads_local),
    )
    own_sum, own_den = (
        lax.psum_scatter(
            summed.astype(jnp.bfloat16), "req", scatter_dimension=0, tiled=True
        ).astype(jnp.float32),
        lax.psum_scatter(
            totals.astype(jnp.bfloat16), "req", scatter_dimension=0, tiled=True
        ).astype(jnp.float32),
    )
    own_top = lax.dynamic_slice_in_dim(global_top, first_request, req_local, 0)
    query_own = queries.reshape(req_local, tree_size, heads_local, head_dim)
    keys_own = keys_new.reshape(req_local, tree_size, heads_local, head_dim)
    values_own = values_new.reshape(req_local, tree_size, heads_local, head_dim)
    tree_scores = jnp.einsum(
        "jqhd,jkhd->jqhk", query_own, keys_own, preferred_element_type=jnp.float32
    )
    tree_mask = (reach > 0)[:, :, None, :]
    tree_scores = jnp.where(tree_mask, tree_scores, NEG_FILL)
    top = jnp.maximum(own_top, jnp.max(tree_scores, axis=3))
    carried = jnp.exp(own_top - top)
    tree_weights = jnp.where(tree_mask, jnp.exp(tree_scores - top[..., None]), 0.0)
    denominator = own_den * carried + jnp.sum(tree_weights, axis=3)
    numerator = own_sum * carried[..., None] + jnp.einsum(
        "jqhk,jkhd->jqhd",
        tree_weights.astype(jnp.bfloat16),
        values_own,
        preferred_element_type=jnp.float32,
    )
    attended = (
        (numerator / denominator[..., None])
        .astype(jnp.bfloat16)
        .reshape(tokens_local, heads_local * head_dim)
    )
    attn_delta = lax.psum_scatter(
        jnp.dot(attended, out_weight, preferred_element_type=jnp.float32).astype(jnp.bfloat16),
        "head",
        scatter_dimension=1,
        tiled=True,
    ).astype(jnp.float32)
    first_streams = remix(stream_vals, hc_mix[0], hc_out[0], attn_delta)
    mixed_mid = blend(first_streams, hc_in[1])
    mid_sum, mid_square = lax.psum(
        (jnp.sum(mixed_mid, axis=1), jnp.sum(mixed_mid * mixed_mid, axis=1)), "head"
    )
    normed_mid = normalize(mixed_mid, mid_sum[:, None], mid_square[:, None], width).astype(
        jnp.bfloat16
    )
    gate_up_flat = up_gate.reshape(width, -1)
    hidden_local = gate_up_flat.shape[1] // 2
    gate_up = fold_rows(gate_up_flat, lax.all_gather(normed_mid, "head", axis=1, tiled=True))
    hidden = (jax.nn.silu(gate_up[:, :hidden_local]) * gate_up[:, hidden_local:]).astype(
        jnp.bfloat16
    )
    mlp_delta = lax.psum_scatter(
        jnp.dot(hidden, down_weight, preferred_element_type=jnp.float32).astype(jnp.bfloat16),
        "head",
        scatter_dimension=1,
        tiled=True,
    ).astype(jnp.float32)
    second_streams = remix(first_streams, hc_mix[1], hc_out[1], mlp_delta)
    new_streams = second_streams.astype(jnp.bfloat16)
    rows_taken = jnp.arange(req_local, dtype=jnp.int32) * tree_size + accepted_index
    final_local = stream_total(second_streams[rows_taken])
    final_full = lax.all_gather(final_local, "head", axis=1, tiled=True)
    final_norm = layer_norm(final_full)
    own_columns = lax.dynamic_slice_in_dim(
        final_norm, lax.axis_index("head") * feature_local, feature_local, 1
    )
    branch = jnp.einsum(
        "jd,kde->jke",
        final_norm.astype(jnp.bfloat16),
        draft_weight,
        preferred_element_type=jnp.float32,
    )
    drafted = (own_columns[:, None, :] + jax.nn.silu(branch)).astype(jnp.bfloat16)
    draft_full = lax.all_gather(drafted, "head", axis=2, tiled=True)
    draft_all = lax.all_gather(draft_full, "req", axis=0, tiled=True)
    logits_local = jnp.dot(
        draft_all.reshape(-1, width), lm_head, preferred_element_type=jnp.float32
    )
    logits_local = logits_local.reshape(all_requests, draft_count, -1)
    logits = lax.all_to_all(
        logits_local.astype(jnp.bfloat16), ("req", "head"), split_axis=0, concat_axis=2, tiled=True
    ).astype(logits_local.dtype)
    return (new_streams, logits)


def solution(mesh):
    in_specs = (
        P("req", None, "head"),
        P(),
        P(),
        P(),
        P(None, None, "head"),
        P("head", None),
        P(None, None, "head"),
        P("head", None),
        P(None, None, "head"),
        P(None, ("req", "head")),
        P("req", None, "head", None),
        P("req", None, "head", None),
        P("req"),
        P("req"),
        P("req"),
        P("req", None),
        P("req"),
    )
    out_specs = (P("req", None, "head"), P(("req", "head"), None, None))
    return jax.shard_map(
        on_device, mesh=mesh, in_specs=in_specs, out_specs=out_specs, check_vma=False
    )
```

profile of v0, /device:TPU:1, one launch (start us, length us, event | category | flops | bytes accessed | tf_op | source)
XLA Modules:
  0.0 640.3 jit_solution(18100017385552382236)
XLA Ops:
  7.2 1.6 fusion.96
  8.9 1.7 copy_convert_fusion
  10.6 1.6 copy-done.2
  12.2 2.8 fusion.92
  16.1 14.7 %all-reduce.2 = (f32[768]{0:T(1024)S(1)}, f32[768]{0:T(1024)S(1)}) all-reduce(f32[768]{0:T(1024)S(1)} %fusion.47, f32[768]{0:T(1024)S(1)} %get-tuple-element.29), channel_id=1, replica_groups=mesh['req'=16,'head'=8] {'head'}, use_global_device_ids=true, to_apply=%region_3.0 | all-reduce | flops 1536 | bytes 12288 | tf_op jit(solution)/shard_map/psum | solution.py:111
  30.8 2.2 fusion.46
  33.0 4.7 copy.195
  40.3 1.3 fusion.97
  41.7 1.5 multiply_cosine_fusion
  43.3 23.3 %all-gather.6.cloned.1.call-done = bf16[768,2048]{1,0:T(8,128)(2,1)} async-done(((bf16[768,256]{1,0:T(8,128)(2,1)}), bf16[768,2048]{1,0:T(8,128)(2,1)}) %all-gather.6.cloned.1.call-update) | async-done | bytes 3145744 | tf_op jit(solution)/shard_map/all_gather | solution.py:118
  66.6 5.5 fusion.1
  72.2 1.0 copy-done.25
  73.6 0.9 subtract_convert_fusion
  76.1 2.0 copy.198
  78.0 2.0 convert_element_type.127
  81.5 60.3 %all-gather.8.cloned.1.call-done = bf16[256,48,256]{2,1,0:T(8,128)(2,1)} async-done(((bf16[16,48,256]{2,1,0:T(8,128)(2,1)}), bf16[256,48,256]{2,1,0:T(8,128)(2,1)}) %all-gather.8.cloned.1.call-update) | async-done | bytes 6291472 | tf_op jit(solution)/shard_map/all_gather | solution.py:123
  141.8 9.1 %copy.199 = bf16[256,48,256]{0,2,1:T(8,128)(2,1)} copy(bf16[256,48,256]{2,1,0:T(8,128)(2,1)} %all-gather.8.cloned.1.call-done) | data formatting | bytes 12582912 | tf_op jit(solution)/shard_map/all_gather | solution.py:123
  150.9 9.1 %copy.200 = bf16[256,48,2,128]{3,1,2,0:T(8,128)(2,1)} copy(bf16[256,48,2,128]{0,3,2,1:T(8,128)(2,1)} %bitcast.193) | data formatting | bytes 12582912 | tf_op jit(solution)/shard_map/reshape | solution.py:126
  160.1 4.5 gather_fusion
  164.6 5.1 bitcast_reduce_fusion
  170.6 58.9 %pmax.7 = bf16[256,48,2]{0,1,2:T(8,128)(2,1)S(1)} all-reduce(bf16[256,48,2]{0,1,2:T(8,128)(2,1)S(1)} %select_reduce_fusion), channel_id=1, replica_groups=mesh['req'=16,'head'=8] {'req'}, use_global_device_ids=true, to_apply=%region_7.8 | all-reduce | flops 24576 | bytes 98304 | tf_op jit(solution)/shard_map/pmax | solution.py:142
  230.2 3.6 fusion.12
  233.8 1.2 copy.204
  235.0 2.9 reshape.384
  238.0 3.3 dot_general.78
  241.3 7.3 %convolution_convert_fusion = bf16[256,48,2,128]{3,0,2,1:T(8,128)(2,1)} fusion(f32[48,2,128,48]{2,1,0,3:T(2,128)S(1)} %dot_general.78, s32[48]{0:T(128)S(1)} %copy-done.30), kind=kOutput, calls=%fused_computation.4 | convolution fusion | flops 1815097344 | bytes 8650944 | tf_op jit(solution)/shard_map/dot_general | solution.py:150
  252.2 1.9 slice.463
  254.1 1.3 copy.209
  255.5 1.3 copy.210
  257.9 1.7 concatenate.21
  259.6 1.2 copy.208
  260.9 3.0 fusion.98
  264.3 1.5 fusion.10
  266.3 57.3 %all-reduce = bf16[256,48,2]{1,2,0:T(2,128)(2,1)S(1)} all-reduce(bf16[256,48,2]{1,2,0:T(2,128)(2,1)S(1)} %copy.220), channel_id=4, replica_groups=mesh['req'=16,'head'=8] {'req'}, use_global_device_ids=true, to_apply=%region_11.12.clone | all-reduce | flops 24576 | bytes 98304
  323.9 1.4 fusion.48
  325.6 1.6 fusion.50
  327.2 12.3 %reduce-scatter.4.cloned.1.call-done = bf16[16,48,2,128]{3,0,2,1:T(8,128)(2,1)} async-done(((bf16[256,48,2,128]{3,0,2,1:T(8,128)(2,1)}), bf16[16,48,2,128]{3,0,2,1:T(8,128)(2,1)}) %reduce-scatter.4.cloned.1.call-update) | async-done | bytes 393232 | tf_op jit(solution)/shard_map/reduce_scatter | solution.py:157
  339.5 1.6 fusion.44
  341.4 2.6 convolution_convert_fusion.2
  346.1 43.6 %reduce-scatter.6.cloned.1.call-done = bf16[768,256]{1,0:T(8,128)(2,1)} async-done(((bf16[768,2048]{1,0:T(8,128)(2,1)}), bf16[768,256]{1,0:T(8,128)(2,1)}) %reduce-scatter.6.cloned.1.call-update) | async-done | bytes 393232 | tf_op jit(solution)/shard_map/reduce_scatter | solution.py:188
  389.7 18.8 %fusion.87 = (f32[768]{0:T(1024)S(1)}, f32[768]{0:T(1024)S(1)}, f32[768,256]{1,0:T(8,128)}, f32[768,256]{1,0:T(8,128)}, f32[768,256]{1,0:T(8,128)}, /*index=5*/f32[768,256]{1,0:T(8,128)}, f32[768,256]{1,0:T(8,128)}) fusion(f32[]{:T(128)} %bitcast.60, f32[]{:T(128)} %bitcast.59, f32[]{:T(128)} %bitcast.58, f32[]{:T(128)} %bitcast.57, ...), kind=kLoop, calls=%fused_computation.157 | loop fusion | flops 9239040 | bytes 7477344 | tf_op jit(solution)/shard_map/reduce_sum | solution.py:197
  408.5 15.9 %all-reduce.1 = (f32[768]{0:T(1024)S(1)}, f32[768]{0:T(1024)S(1)}) all-reduce(f32[768]{0:T(1024)S(1)} %get-tuple-element.17, f32[768]{0:T(1024)S(1)} %get-tuple-element.16), channel_id=1, replica_groups=mesh['req'=16,'head'=8] {'head'}, use_global_device_ids=true, to_apply=%region_17.18 | all-reduce | flops 1536 | bytes 12288 | tf_op jit(solution)/shard_map/psum | solution.py:196
  424.5 2.2 multiply_convert_fusion
  427.1 10.2 %copy.237 = bf16[256,8,2,1024]{3,1,2,0:T(8,128)(2,1)} copy(bf16[256,8,2,1024]{3,2,1,0:T(2,128)(2,1)} %bitcast.195) | data formatting | bytes 16777216
  437.3 20.8 %all-gather.10.cloned.1.call-done = bf16[768,2048]{1,0:T(8,128)(2,1)} async-done(((bf16[768,256]{1,0:T(8,128)(2,1)}), bf16[768,2048]{1,0:T(8,128)(2,1)}) %all-gather.10.cloned.1.call-update) | async-done | bytes 3145744 | tf_op jit(solution)/shard_map/all_gather | solution.py:204
  458.0 10.1 %fusion.99 = f32[768,2048]{1,0:T(8,128)S(1)} fusion(bf16[768,2048]{1,0:T(8,128)(2,1)} %all-gather.10.cloned.1.call-done, bf16[2048,2048]{1,0:T(8,128)(2,1)} %bitcast.196), kind=kOutput, calls=%fused_computation.165 | convolution fusion | flops 6442450944 | bytes 17825792 | tf_op jit(solution)/shard_map/dot_general | solution.py:73
  468.2 4.9 convolution_convert_fusion.1
  474.5 31.9 %reduce-scatter.8.cloned.1.call-done = bf16[768,256]{1,0:T(8,128)(2,1)} async-done(((bf16[768,2048]{1,0:T(8,128)(2,1)}), bf16[768,256]{1,0:T(8,128)(2,1)}) %reduce-scatter.8.cloned.1.call-update) | async-done | bytes 393232 | tf_op jit(solution)/shard_map/reduce_scatter | solution.py:208
  506.5 7.7 %fusion.34 = (f32[768,1,256]{2,0,1:T(8,128)S(1)}, f32[768,1,256]{2,0,1:T(8,128)S(1)}) fusion(bf16[768,256]{1,0:T(8,128)(2,1)} %reduce-scatter.8.cloned.1.call-done, f32[768,256]{1,0:T(8,128)S(1)} %copy-done.8, f32[768,256]{1,0:T(8,128)S(1)} %copy-done.7, f32[768,256]{1,0:T(8,128)S(1)} %copy-done.6, f32[768,256]{1,0:T(8,128)S(1)} %copy-done.5, f32[]{:T(128)} %bitcast.56, ...), kind=kLoop, calls=%fused_computation.57 | loop fusion | flops 3735552 | bytes 5111848 | tf_op jit(solution)/shard_map/stack | solution.py:62
  514.2 6.8 %fusion.38 = (f32[768,1,256]{2,0,1:T(8,128)S(1)}, f32[768,1,256]{2,0,1:T(8,128)S(1)}) fusion(bf16[768,256]{1,0:T(8,128)(2,1)S(1)} %copy-done.21, f32[768,256]{1,0:T(8,128)S(1)} %copy-done.8, f32[768,256]{1,0:T(8,128)S(1)} %copy-done.7, f32[768,256]{1,0:T(8,128)S(1)} %copy-done.6, f32[768,256]{1,0:T(8,128)S(1)} %copy-done.5, f32[]{:T(128)} %bitcast.72, ...), kind=kLoop, calls=%fused_computation.61 | loop fusion | flops 3735552 | bytes 5111848 | tf_op jit(solution)/shard_map/stack | solution.py:62
  522.3 3.7 copy.225
  525.9 2.5 gather_fusion.2
  528.5 12.1 %all-gather = f32[16,1,2048]{2,1,0:T(1,128)S(1)} all-gather(f32[16,1,256]{2,1,0:T(1,128)S(1)} %slice_add_fusion), channel_id=2, replica_groups=mesh['req'=16,'head'=8] {'head'}, dimensions={2}, use_global_device_ids=true | all-gather | bytes 147456 | tf_op jit(solution)/shard_map/all_gather | solution.py:218
  541.1 2.0 add_convert_fusion.1
  543.1 13.9 %all_gather.22 = bf16[16,2,2048]{2,0,1:T(8,128)(2,1)} all-gather(bf16[16,2,256]{2,0,1:T(8,128)(2,1)S(1)} %add_convert_fusion.1), channel_id=1, replica_groups=mesh['req'=16,'head'=8] {'head'}, dimensions={2}, use_global_device_ids=true | all-gather | bytes 147456 | tf_op jit(solution)/shard_map/all_gather | solution.py:230
  557.1 43.6 %all-gather.12.cloned.1.call-done = bf16[256,2,2048]{2,0,1:T(8,128)(2,1)} async-done(((bf16[16,2,2048]{2,0,1:T(8,128)(2,1)}), bf16[256,2,2048]{2,0,1:T(8,128)(2,1)}) %all-gather.12.cloned.1.call-update) | async-done | bytes 2097168 | tf_op jit(solution)/shard_map/all_gather | solution.py:231
  600.8 3.1 fusion.20
  603.9 1.2 copy.226
  605.0 9.0 %all-to-all-start = ((bf16[256,2,393]{2,1,0:T(2,128)(2,1)}), bf16[256,2,393]{2,1,0:T(2,128)(2,1)}, u32[]{:S(2)}, u32[]{:S(2)}) async-start(bf16[256,2,393]{2,1,0:T(2,128)(2,1)} %copy.226), calls=%async_computation.3 | async-start | bytes 1048576 | tf_op jit(solution)/shard_map/all_to_all | solution.py:236
  614.4 2.4 copy.228
  616.8 10.5 %all-to-all-done = bf16[256,2,393]{2,1,0:T(2,128)(2,1)} async-done(((bf16[256,2,393]{2,1,0:T(2,128)(2,1)}), bf16[256,2,393]{2,1,0:T(2,128)(2,1)}, u32[]{:S(2)}, u32[]{:S(2)}) %all-to-all-start) | async-done | bytes 402464 | tf_op jit(solution)/shard_map/all_to_all | solution.py:236
  627.3 1.4 convert_bitcast_fusion
  628.7 1.3 copy.227
  630.1 3.2 reshape.388
  (143 shorter events, 20.7 us)
Async XLA Ops:
  7.2 157.5 %copy-start = (bf16[48,128,2,128]{3,2,1,0:T(2,128)(2,1)S(1)}, bf16[48,128,2,128]{3,2,1,0:T(2,128)(2,1)}, u32[]{:S(2)}) copy-start(bf16[48,128,2,128]{3,2,1,0:T(2,128)(2,1)} %param.27) | copy-start | bytes 9437188
  7.2 59.4 %all-gather.6.cloned.1.call-start = ((), (), s32[]{:S(2)}) async-start(), calls=%async_computation.4 | async-start | bytes 3538944 | tf_op jit(solution)/shard_map/all_gather | solution.py:118
  10.5 1.6 copy-start.2
  15.0 0.9 copy-start.17
  33.0 4.8 copy-start.34
  33.0 108.8 %all-gather.8.cloned.1.call-start = ((), (), s32[]{:S(2)}) async-start(), calls=%async_computation.5 | async-start | bytes 6684672 | tf_op jit(solution)/shard_map/all_gather | solution.py:123
  37.8 3.8 copy-start.32
  72.1 2.4 copy-start.20
  72.1 1.1 copy-start.25
  72.1 1.5 copy-start.26
  73.6 6.5 %copy-start.30 = (s32[48]{0:T(128)S(1)}, s32[48]{0:T(128)}, u32[]{:S(2)}) copy-start(s32[48]{0:T(128)} %param.29) | copy-start | bytes 580
  74.5 0.7 copy-start.18
  80.0 259.5 %reduce-scatter.4.cloned.1.call-start = ((), (), s32[]{:S(2)}) async-start(), calls=%async_computation.6 | async-start | bytes 6684672 | tf_op jit(solution)/shard_map/reduce_scatter | solution.py:157
  164.6 5.1 copy-start.28
  248.6 1.0 copy-start.23
  248.6 1.3 copy-start.36
  248.6 2.5 copy-start.19
  248.6 141.2 %reduce-scatter.6.cloned.1.call-start = ((), (), s32[]{:S(2)}) async-start(), calls=%async_computation.7 | async-start | bytes 3538944 | tf_op jit(solution)/shard_map/reduce_scatter | solution.py:188
  251.6 5.2 copy-start.27
  257.9 6.3 copy-start.4
  260.9 3.1 copy-start.22
  323.6 17.8 %copy-start.24 = (bf16[256,2048]{1,0:T(8,128)(2,1)S(1)}, bf16[256,2048]{1,0:T(8,128)(2,1)}, u32[]{:S(2)}) copy-start(bf16[256,2048]{1,0:T(8,128)(2,1)} %param.22) | copy-start | bytes 3145732
  344.1 0.7 copy-start.29
  344.1 1.4 copy-start.31
  344.1 45.7 %copy-start.3 = (f32[768,4,256]{2,0,1:T(8,128)S(1)}, f32[768,4,256]{2,0,1:T(8,128)}, u32[]{:S(2)}) copy-start(f32[768,4,256]{2,0,1:T(8,128)} %copy-done.2) | copy-start | bytes 9437188
  344.1 113.9 %all-gather.10.cloned.1.call-start = ((), (), s32[]{:S(2)}) async-start(), calls=%async_computation.8 | async-start | bytes 3538944 | tf_op jit(solution)/shard_map/all_gather | solution.py:204
  426.7 79.8 %reduce-scatter.8.cloned.1.call-start = ((), (), s32[]{:S(2)}) async-start(), calls=%async_computation.9 | async-start | bytes 3538944 | tf_op jit(solution)/shard_map/reduce_scatter | solution.py:208
  458.0 10.2 %copy-start.33 = (bf16[1024,2048]{1,0:T(8,128)(2,1)S(1)}, bf16[1024,2048]{1,0:T(8,128)(2,1)}, u32[]{:S(2)}) copy-start(bf16[1024,2048]{1,0:T(8,128)(2,1)} %param.24) | copy-start | bytes 12582916
  473.1 0.7 copy-start.35
  473.1 33.3 %copy-start.5 = (f32[768,256]{1,0:T(8,128)S(1)}, f32[768,256]{1,0:T(8,128)}, u32[]{:S(2)}) copy-start(f32[768,256]{1,0:T(8,128)} %get-tuple-element.23) | copy-start | bytes 2359300
  473.1 33.3 %copy-start.6 = (f32[768,256]{1,0:T(8,128)S(1)}, f32[768,256]{1,0:T(8,128)}, u32[]{:S(2)}) copy-start(f32[768,256]{1,0:T(8,128)} %get-tuple-element.24) | copy-start | bytes 2359300
  473.1 33.3 %copy-start.7 = (f32[768,256]{1,0:T(8,128)S(1)}, f32[768,256]{1,0:T(8,128)}, u32[]{:S(2)}) copy-start(f32[768,256]{1,0:T(8,128)} %get-tuple-element.25) | copy-start | bytes 2359300
  473.1 33.3 %copy-start.8 = (f32[768,256]{1,0:T(8,128)S(1)}, f32[768,256]{1,0:T(8,128)}, u32[]{:S(2)}) copy-start(f32[768,256]{1,0:T(8,128)} %get-tuple-element.26) | copy-start | bytes 2359300
  473.2 127.6 %all-gather.12.cloned.1.call-start = ((), (), s32[]{:S(2)}) async-start(), calls=%async_computation.10 | async-start | bytes 2228224 | tf_op jit(solution)/shard_map/all_gather | solution.py:231
  506.4 7.7 %copy-start.21 = (bf16[768,256]{1,0:T(8,128)(2,1)S(1)}, bf16[768,256]{1,0:T(8,128)(2,1)}, u32[]{:S(2)}) copy-start(bf16[768,256]{1,0:T(8,128)(2,1)} %reduce-scatter.8.cloned.1.call-done) | copy-start | bytes 1179652
  514.1 6.8 %copy-start.9 = (f32[768,1,256]{2,0,1:T(8,128)}, f32[768,1,256]{2,0,1:T(8,128)S(1)}, u32[]{:S(2)}) copy-start(f32[768,1,256]{2,0,1:T(8,128)S(1)} %get-tuple-element.31) | copy-start | bytes 2359300
  514.1 6.8 %copy-start.11 = (f32[768,1,256]{2,0,1:T(8,128)}, f32[768,1,256]{2,0,1:T(8,128)S(1)}, u32[]{:S(2)}) copy-start(f32[768,1,256]{2,0,1:T(8,128)S(1)} %get-tuple-element.32) | copy-start | bytes 2359300
  520.9 0.9 copy-start.13
  521.0 1.1 copy-start.15
  557.1 57.0 %copy-start.10 = (f32[768,1,256]{2,0,1:T(8,128)S(1)}, f32[768,1,256]{2,0,1:T(8,128)}, u32[]{:S(2)}) copy-start(f32[768,1,256]{2,0,1:T(8,128)} %copy-done.9) | copy-start | bytes 2359300
  557.1 57.0 %copy-start.12 = (f32[768,1,256]{2,0,1:T(8,128)S(1)}, f32[768,1,256]{2,0,1:T(8,128)}, u32[]{:S(2)}) copy-start(f32[768,1,256]{2,0,1:T(8,128)} %copy-done.11) | copy-start | bytes 2359300
  557.1 57.0 %copy-start.14 = (f32[768,1,256]{2,0,1:T(8,128)S(1)}, f32[768,1,256]{2,0,1:T(8,128)}, u32[]{:S(2)}) copy-start(f32[768,1,256]{2,0,1:T(8,128)} %copy-done.13) | copy-start | bytes 2359300
  557.1 57.0 %copy-start.16 = (f32[768,1,256]{2,0,1:T(8,128)S(1)}, f32[768,1,256]{2,0,1:T(8,128)}, u32[]{:S(2)}) copy-start(f32[768,1,256]{2,0,1:T(8,128)} %copy-done.15) | copy-start | bytes 2359300
  605.0 22.3 %all-to-all-start = ((bf16[256,2,393]{2,1,0:T(2,128)(2,1)}), bf16[256,2,393]{2,1,0:T(2,128)(2,1)}, u32[]{:S(2)}, u32[]{:S(2)}) async-start(bf16[256,2,393]{2,1,0:T(2,128)(2,1)} %copy.226), calls=%async_computation.3 | async-start | bytes 1048576 | tf_op jit(solution)/shard_map/all_to_all | solution.py:236
  614.4 18.8 %copy-start.1 = (bf16[48,128,2,128]{3,2,1,0:T(2,128)(2,1)S(1)}, bf16[48,128,2,128]{3,2,1,0:T(2,128)(2,1)}, u32[]{:S(2)}) copy-start(bf16[48,128,2,128]{3,2,1,0:T(2,128)(2,1)} %param.27) | copy-start | bytes 9437188
Sparse Core Ops, SparseCore 0:
  33.1 33.4 all-gather.5
  80.1 61.6 all-gather.7
  248.7 90.7 reduce-scatter.3
  344.2 45.4 reduce-scatter.5
  426.8 31.2 all-gather.9
  473.3 33.1 reduce-scatter.7
  557.2 43.5 all-gather.11
where the time goes:
time: 650 us; the launch traced here: 640 us
  waiting for transfers between devices  246 us (38%)
  blocking collectives  173 us (27%)
  local copies, waits for them, and re-layouts  87.2 us (13%)
  other arithmetic  55.1 us (8%)
  matrix products  53.1 us (8%)
  between operations  15.7 us (2%)
  starting transfers between devices  9.87 us (2%)
    all_gather x1, waiting for transfers between devices, on_device(): lax.all_gather(queries.reshape(req_local, tree_size, heads_local * head_d...  60.3 us
    pmax x1, blocking collectives, on_device(): lax.pmax(local_top.astype(jnp.bfloat16), 'req').astype(local_top.dtype)  58.9 us
    unnamed x1, blocking collectives  57.3 us
    all_gather x1, waiting for transfers between devices, on_device(): draft_all = lax.all_gather(draft_full, 'req', axis=0, tiled=True)  43.6 us
    reduce_scatter x1, waiting for transfers between devices, on_device(): lax.psum_scatter(jnp.dot(attended, out_weight, preferred_element_type=jnp...  43.6 us
    reduce_scatter x1, waiting for transfers between devices, on_device(): lax.psum_scatter(jnp.dot(hidden, down_weight, preferred_element_type=jnp....  31.9 us
    unnamed x79, local copies, waits for them, and re-layouts  25.5 us
    all_gather x1, waiting for transfers between devices, on_device(): lax.all_gather(normed, 'head', axis=1, tiled=True)  23.3 us
  transfers between devices with their start and end apart: 8, of which 8 were waited for; matrix products, arithmetic and copies ran while one was open for 7% of the time, Pallas kernels for 0%

commit v1 on v0

--- a/solution.py
+++ b/solution.py
@@ -227,7 +227,12 @@
         preferred_element_type=jnp.float32,
     )
     drafted = (own_columns[:, None, :] + jax.nn.silu(branch)).astype(jnp.bfloat16)
-    draft_full = lax.all_gather(drafted, "head", axis=2, tiled=True)
+    ring = [drafted]
+    for hop in range(7):
+        ring.append(lax.ppermute(ring[-1], "head", [(dev, (dev + 1) % 8) for dev in range(8)]))
+    draft_full = jnp.roll(
+        jnp.concatenate(ring[::-1], axis=2), (lax.axis_index("head") + 1) * ring[0].shape[2], axis=2
+    )
     draft_all = lax.all_gather(draft_full, "req", axis=0, tiled=True)
     logits_local = jnp.dot(
         draft_all.reshape(-1, width), lm_head, preferred_element_type=jnp.float32

time: 650 us -> 667 us (1.026)
  waiting for transfers between devices: 246 us -> 267 us
  blocking collectives: 173 us -> 159 us
  starting transfers between devices: 9.87 us -> 18.3 us
    ppermute x0 -> x7, waiting for transfers between devices: none -> 18.7 us  [on_device(): lax.ppermute(ring[-1], 'head', [(dev, (dev + 1) % 8) for dev in range(8)])]
    all_gather x1 -> x0, blocking collectives: 13.9 us -> none  [on_device(): draft_full = lax.all_gather(drafted, 'head', axis=2, tiled=True)]
    ppermute x0 -> x7, starting transfers between devices: none -> 8.44 us  [on_device(): lax.ppermute(ring[-1], 'head', [(dev, (dev + 1) % 8) for dev in range(8)])]
    unnamed x79 -> x96, local copies, waits for them, and re-layouts: 25.5 us -> 25 us
  transfers between devices with their start and end apart: 8 -> 15, of which waited for: 8 -> 15; matrix products, arithmetic and copies ran while one was open for 7% -> 7% of each run, Pallas kernels for 0% -> 0%
where the time goes in v1:
time: 667 us; the launch traced here: 657 us
  waiting for transfers between devices  267 us (40%)
  blocking collectives  159 us (24%)
  local copies, waits for them, and re-layouts  87.5 us (13%)
  other arithmetic  56.3 us (8%)
  matrix products  53 us (8%)
  starting transfers between devices  18.3 us (3%)
  between operations  15.8 us (2%)
    all_gather x1, waiting for transfers between devices, on_device(): lax.all_gather(queries.reshape(req_local, tree_size, heads_local * head_d...  59.6 us
    pmax x1, blocking collectives, on_device(): lax.pmax(local_top.astype(jnp.bfloat16), 'req').astype(local_top.dtype)  58.9 us
    unnamed x1, blocking collectives  57.4 us
    all_gather x1, waiting for transfers between devices, on_device(): draft_all = lax.all_gather(draft_full, 'req', axis=0, tiled=True)  45.8 us
    reduce_scatter x1, waiting for transfers between devices, on_device(): lax.psum_scatter(jnp.dot(attended, out_weight, preferred_element_type=jnp...  43.6 us
    reduce_scatter x1, waiting for transfers between devices, on_device(): lax.psum_scatter(jnp.dot(hidden, down_weight, preferred_element_type=jnp....  32.5 us
    unnamed x96, local copies, waits for them, and re-layouts  25 us
    all_gather x1, waiting for transfers between devices, on_device(): lax.all_gather(normed, 'head', axis=1, tiled=True)  23.3 us
  transfers between devices with their start and end apart: 15, of which 15 were waited for; matrix products, arithmetic and copies ran while one was open for 7% of the time, Pallas kernels for 0%

profile of v1, /device:TPU:1, one launch (start us, length us, event | category | flops | bytes accessed | tf_op | source)
XLA Modules:
  0.0 657.2 jit_solution(7461773020739437105)
XLA Ops:
  7.2 1.7 fusion.96
  8.9 1.7 copy_convert_fusion
  10.6 1.6 copy-done.2
  12.2 2.8 fusion.92
  16.0 14.7 %all-reduce.2 = (f32[768]{0:T(1024)S(1)}, f32[768]{0:T(1024)S(1)}) all-reduce(f32[768]{0:T(1024)S(1)} %fusion.47, f32[768]{0:T(1024)S(1)} %get-tuple-element.29), channel_id=1, replica_groups=mesh['req'=16,'head'=8] {'head'}, use_global_device_ids=true, to_apply=%region_3.0 | all-reduce | flops 1536 | bytes 12288 | tf_op jit(solution)/shard_map/psum | solution.py:111
  30.7 2.2 fusion.46
  33.0 4.7 copy.195
  41.7 1.5 multiply_cosine_fusion
  43.2 23.3 %all-gather.6.cloned.1.call-done = bf16[768,2048]{1,0:T(8,128)(2,1)} async-done(((bf16[768,256]{1,0:T(8,128)(2,1)}), bf16[768,2048]{1,0:T(8,128)(2,1)}) %all-gather.6.cloned.1.call-update) | async-done | bytes 3145744 | tf_op jit(solution)/shard_map/all_gather | solution.py:118
  66.6 5.5 fusion.1
  76.0 2.0 copy.198
  78.0 2.0 convert_element_type.127
  82.2 59.6 %all-gather.8.cloned.1.call-done = bf16[256,48,256]{2,1,0:T(8,128)(2,1)} async-done(((bf16[16,48,256]{2,1,0:T(8,128)(2,1)}), bf16[256,48,256]{2,1,0:T(8,128)(2,1)}) %all-gather.8.cloned.1.call-update) | async-done | bytes 6291472 | tf_op jit(solution)/shard_map/all_gather | solution.py:123
  141.8 9.2 %copy.199 = bf16[256,48,256]{0,2,1:T(8,128)(2,1)} copy(bf16[256,48,256]{2,1,0:T(8,128)(2,1)} %all-gather.8.cloned.1.call-done) | data formatting | bytes 12582912 | tf_op jit(solution)/shard_map/all_gather | solution.py:123
  151.0 9.2 %copy.200 = bf16[256,48,2,128]{3,1,2,0:T(8,128)(2,1)} copy(bf16[256,48,2,128]{0,3,2,1:T(8,128)(2,1)} %bitcast.193) | data formatting | bytes 12582912 | tf_op jit(solution)/shard_map/reshape | solution.py:126
  160.2 4.5 gather_fusion
  164.7 5.1 bitcast_reduce_fusion
  170.6 58.9 %pmax.7 = bf16[256,48,2]{0,1,2:T(8,128)(2,1)S(1)} all-reduce(bf16[256,48,2]{0,1,2:T(8,128)(2,1)S(1)} %select_reduce_fusion), channel_id=1, replica_groups=mesh['req'=16,'head'=8] {'req'}, use_global_device_ids=true, to_apply=%region_7.8 | all-reduce | flops 24576 | bytes 98304 | tf_op jit(solution)/shard_map/pmax | solution.py:142
  230.2 3.6 fusion.12
  235.1 2.9 reshape.384
  238.0 3.3 dot_general.78
  241.4 7.3 %convolution_convert_fusion = bf16[256,48,2,128]{3,0,2,1:T(8,128)(2,1)} fusion(f32[48,2,128,48]{2,1,0,3:T(2,128)S(1)} %dot_general.78, s32[48]{0:T(128)S(1)} %copy-done.31), kind=kOutput, calls=%fused_computation.4 | convolution fusion | flops 1815097344 | bytes 8650944 | tf_op jit(solution)/shard_map/dot_general | solution.py:150
  252.3 2.0 slice.463
  254.2 1.3 copy.209
  258.1 1.7 concatenate.27
  261.0 3.0 fusion.98
  264.3 1.5 fusion.10
  266.4 57.4 %all-reduce = bf16[256,48,2]{1,2,0:T(2,128)(2,1)S(1)} all-reduce(bf16[256,48,2]{1,2,0:T(2,128)(2,1)S(1)} %copy.220), channel_id=4, replica_groups=mesh['req'=16,'head'=8] {'req'}, use_global_device_ids=true, to_apply=%region_11.12.clone | all-reduce | flops 24576 | bytes 98304
  324.1 1.4 fusion.48
  325.7 1.6 fusion.50
  327.4 12.3 %reduce-scatter.4.cloned.1.call-done = bf16[16,48,2,128]{3,0,2,1:T(8,128)(2,1)} async-done(((bf16[256,48,2,128]{3,0,2,1:T(8,128)(2,1)}), bf16[16,48,2,128]{3,0,2,1:T(8,128)(2,1)}) %reduce-scatter.4.cloned.1.call-update) | async-done | bytes 393232 | tf_op jit(solution)/shard_map/reduce_scatter | solution.py:157
  339.6 1.6 fusion.44
  341.6 2.6 convolution_convert_fusion.2
  346.3 43.6 %reduce-scatter.6.cloned.1.call-done = bf16[768,256]{1,0:T(8,128)(2,1)} async-done(((bf16[768,2048]{1,0:T(8,128)(2,1)}), bf16[768,256]{1,0:T(8,128)(2,1)}) %reduce-scatter.6.cloned.1.call-update) | async-done | bytes 393232 | tf_op jit(solution)/shard_map/reduce_scatter | solution.py:188
  389.9 19.1 %fusion.87 = (f32[768]{0:T(1024)S(1)}, f32[768]{0:T(1024)S(1)}, f32[768,256]{1,0:T(8,128)}, f32[768,256]{1,0:T(8,128)}, f32[768,256]{1,0:T(8,128)}, /*index=5*/f32[768,256]{1,0:T(8,128)}, f32[768,256]{1,0:T(8,128)}) fusion(f32[]{:T(128)} %bitcast.60, f32[]{:T(128)} %bitcast.59, f32[]{:T(128)} %bitcast.58, f32[]{:T(128)} %bitcast.57, ...), kind=kLoop, calls=%fused_computation.174 | loop fusion | flops 9239040 | bytes 7477344 | tf_op jit(solution)/shard_map/reduce_sum | solution.py:197
  409.0 15.9 %all-reduce.1 = (f32[768]{0:T(1024)S(1)}, f32[768]{0:T(1024)S(1)}) all-reduce(f32[768]{0:T(1024)S(1)} %get-tuple-element.17, f32[768]{0:T(1024)S(1)} %get-tuple-element.16), channel_id=1, replica_groups=mesh['req'=16,'head'=8] {'head'}, use_global_device_ids=true, to_apply=%region_17.18 | all-reduce | flops 1536 | bytes 12288 | tf_op jit(solution)/shard_map/psum | solution.py:196
  424.9 2.1 multiply_convert_fusion
  427.6 10.2 %copy.237 = bf16[256,8,2,1024]{3,1,2,0:T(8,128)(2,1)} copy(bf16[256,8,2,1024]{3,2,1,0:T(2,128)(2,1)} %bitcast.195) | data formatting | bytes 16777216
  437.8 20.9 %all-gather.10.cloned.1.call-done = bf16[768,2048]{1,0:T(8,128)(2,1)} async-done(((bf16[768,256]{1,0:T(8,128)(2,1)}), bf16[768,2048]{1,0:T(8,128)(2,1)}) %all-gather.10.cloned.1.call-update) | async-done | bytes 3145744 | tf_op jit(solution)/shard_map/all_gather | solution.py:204
  458.6 10.2 %fusion.99 = f32[768,2048]{1,0:T(8,128)S(1)} fusion(bf16[768,2048]{1,0:T(8,128)(2,1)} %all-gather.10.cloned.1.call-done, bf16[2048,2048]{1,0:T(8,128)(2,1)} %bitcast.196), kind=kOutput, calls=%fused_computation.182 | convolution fusion | flops 6442450944 | bytes 17825792 | tf_op jit(solution)/shard_map/dot_general | solution.py:73
  468.8 4.9 convolution_convert_fusion.1
  474.6 32.5 %reduce-scatter.8.cloned.1.call-done = bf16[768,256]{1,0:T(8,128)(2,1)} async-done(((bf16[768,2048]{1,0:T(8,128)(2,1)}), bf16[768,256]{1,0:T(8,128)(2,1)}) %reduce-scatter.8.cloned.1.call-update) | async-done | bytes 393232 | tf_op jit(solution)/shard_map/reduce_scatter | solution.py:208
  507.0 7.8 %fusion.34 = (f32[768,1,256]{2,0,1:T(8,128)S(1)}, f32[768,1,256]{2,0,1:T(8,128)S(1)}) fusion(bf16[768,256]{1,0:T(8,128)(2,1)} %reduce-scatter.8.cloned.1.call-done, f32[768,256]{1,0:T(8,128)S(1)} %copy-done.16, f32[768,256]{1,0:T(8,128)S(1)} %copy-done.15, f32[768,256]{1,0:T(8,128)S(1)} %copy-done.14, f32[768,256]{1,0:T(8,128)S(1)} %copy-done.13, ...), kind=kLoop, calls=%fused_computation.57 | loop fusion | flops 3735552 | bytes 5111848 | tf_op jit(solution)/shard_map/stack | solution.py:62
  514.9 6.9 %fusion.38 = (f32[768,1,256]{2,0,1:T(8,128)S(1)}, f32[768,1,256]{2,0,1:T(8,128)S(1)}) fusion(bf16[768,256]{1,0:T(8,128)(2,1)S(1)} %copy-done.21, f32[768,256]{1,0:T(8,128)S(1)} %copy-done.16, f32[768,256]{1,0:T(8,128)S(1)} %copy-done.15, f32[768,256]{1,0:T(8,128)S(1)} %copy-done.14, f32[768,256]{1,0:T(8,128)S(1)} %copy-done.13, f32[]{:T(128)} %bitcast.72, ...), kind=kLoop, calls=%fused_computation.61 | loop fusion | flops 3735552 | bytes 5111848 | tf_op jit(solution)/shard_map/stack | solution.py:62
  523.1 3.7 copy.225
  526.8 2.5 gather_fusion.2
  529.3 12.1 %all-gather = f32[16,1,2048]{2,1,0:T(1,128)S(1)} all-gather(f32[16,1,256]{2,1,0:T(1,128)S(1)} %slice_add_fusion), channel_id=2, replica_groups=mesh['req'=16,'head'=8] {'head'}, dimensions={2}, use_global_device_ids=true | all-gather | bytes 147456 | tf_op jit(solution)/shard_map/all_gather | solution.py:218
  541.9 2.0 add_convert_fusion.1
  543.9 1.8 collective-permute-start
  546.6 2.3 collective-permute-start.1
  549.7 2.3 collective-permute-start.2
  552.0 1.5 collective-permute-done.2
  553.5 1.6 collective-permute-start.3
  555.2 2.7 collective-permute-done.3
  558.4 3.9 collective-permute-done.4
  562.3 4.4 collective-permute-done.5
  566.7 4.4 collective-permute-done.6
  571.9 45.8 %all-gather.12.cloned.1.call-done = bf16[256,2,2048]{2,0,1:T(8,128)(2,1)} async-done(((bf16[16,2,2048]{2,0,1:T(8,128)(2,1)}), bf16[256,2,2048]{2,0,1:T(8,128)(2,1)}) %all-gather.12.cloned.1.call-update) | async-done | bytes 2097168 | tf_op jit(solution)/shard_map/all_gather | solution.py:236
  617.7 3.1 fusion.20
  622.0 9.0 %all-to-all-start = ((bf16[256,2,393]{2,1,0:T(2,128)(2,1)}), bf16[256,2,393]{2,1,0:T(2,128)(2,1)}, u32[]{:S(2)}, u32[]{:S(2)}) async-start(bf16[256,2,393]{2,1,0:T(2,128)(2,1)} %copy.226), calls=%async_computation.3 | async-start | bytes 1048576 | tf_op jit(solution)/shard_map/all_to_all | solution.py:241
  631.4 2.4 copy.228
  633.8 10.5 %all-to-all-done = bf16[256,2,393]{2,1,0:T(2,128)(2,1)} async-done(((bf16[256,2,393]{2,1,0:T(2,128)(2,1)}), bf16[256,2,393]{2,1,0:T(2,128)(2,1)}, u32[]{:S(2)}, u32[]{:S(2)}) %all-to-all-start) | async-done | bytes 402464 | tf_op jit(solution)/shard_map/all_to_all | solution.py:241
  644.3 1.4 convert_bitcast_fusion
  647.0 3.2 reshape.388
  (174 shorter events, 33.1 us)
Async XLA Ops:
  7.2 157.5 %copy-start = (bf16[48,128,2,128]{3,2,1,0:T(2,128)(2,1)S(1)}, bf16[48,128,2,128]{3,2,1,0:T(2,128)(2,1)}, u32[]{:S(2)}) copy-start(bf16[48,128,2,128]{3,2,1,0:T(2,128)(2,1)} %param.27) | copy-start | bytes 9437188
  7.2 59.4 %all-gather.6.cloned.1.call-start = ((), (), s32[]{:S(2)}) async-start(), calls=%async_computation.4 | async-start | bytes 3538944 | tf_op jit(solution)/shard_map/all_gather | solution.py:118
  10.6 1.6 copy-start.2
  15.0 0.9 copy-start.17
  32.9 4.8 copy-start.35
  32.9 108.8 %all-gather.8.cloned.1.call-start = ((), (), s32[]{:S(2)}) async-start(), calls=%async_computation.5 | async-start | bytes 6684672 | tf_op jit(solution)/shard_map/all_gather | solution.py:123
  37.7 3.8 copy-start.33
  72.0 2.4 copy-start.20
  72.1 1.1 copy-start.25
  72.1 1.5 copy-start.26
  73.5 6.5 copy-start.30
  73.5 6.5 copy-start.36
  74.5 0.7 copy-start.18
  80.0 259.7 %reduce-scatter.4.cloned.1.call-start = ((), (), s32[]{:S(2)}) async-start(), calls=%async_computation.6 | async-start | bytes 6684672 | tf_op jit(solution)/shard_map/reduce_scatter | solution.py:157
  164.7 5.1 copy-start.28
  238.0 3.3 copy-start.31
  248.6 1.0 copy-start.23
  248.6 1.3 copy-start.37
  248.7 2.5 copy-start.19
  248.7 141.2 %reduce-scatter.6.cloned.1.call-start = ((), (), s32[]{:S(2)}) async-start(), calls=%async_computation.7 | async-start | bytes 3538944 | tf_op jit(solution)/shard_map/reduce_scatter | solution.py:188
  251.7 5.2 copy-start.27
  258.1 6.3 copy-start.4
  261.0 3.1 copy-start.22
  323.8 17.8 %copy-start.24 = (bf16[256,2048]{1,0:T(8,128)(2,1)S(1)}, bf16[256,2048]{1,0:T(8,128)(2,1)}, u32[]{:S(2)}) copy-start(bf16[256,2048]{1,0:T(8,128)(2,1)} %param.22) | copy-start | bytes 3145732
  344.2 0.7 copy-start.29
  344.2 1.3 copy-start.32
  344.2 45.7 %copy-start.3 = (f32[768,4,256]{2,0,1:T(8,128)S(1)}, f32[768,4,256]{2,0,1:T(8,128)}, u32[]{:S(2)}) copy-start(f32[768,4,256]{2,0,1:T(8,128)} %copy-done.2) | copy-start | bytes 9437188
  344.2 114.4 %all-gather.10.cloned.1.call-start = ((), (), s32[]{:S(2)}) async-start(), calls=%async_computation.8 | async-start | bytes 3538944 | tf_op jit(solution)/shard_map/all_gather | solution.py:204
  427.1 79.9 %reduce-scatter.8.cloned.1.call-start = ((), (), s32[]{:S(2)}) async-start(), calls=%async_computation.9 | async-start | bytes 3538944 | tf_op jit(solution)/shard_map/reduce_scatter | solution.py:208
  458.6 10.2 %copy-start.34 = (bf16[1024,2048]{1,0:T(8,128)(2,1)S(1)}, bf16[1024,2048]{1,0:T(8,128)(2,1)}, u32[]{:S(2)}) copy-start(bf16[1024,2048]{1,0:T(8,128)(2,1)} %param.24) | copy-start | bytes 12582916
  473.7 33.3 %copy-start.13 = (f32[768,256]{1,0:T(8,128)S(1)}, f32[768,256]{1,0:T(8,128)}, u32[]{:S(2)}) copy-start(f32[768,256]{1,0:T(8,128)} %get-tuple-element.23) | copy-start | bytes 2359300
  473.7 33.3 %copy-start.14 = (f32[768,256]{1,0:T(8,128)S(1)}, f32[768,256]{1,0:T(8,128)}, u32[]{:S(2)}) copy-start(f32[768,256]{1,0:T(8,128)} %get-tuple-element.24) | copy-start | bytes 2359300
  473.7 33.3 %copy-start.15 = (f32[768,256]{1,0:T(8,128)S(1)}, f32[768,256]{1,0:T(8,128)}, u32[]{:S(2)}) copy-start(f32[768,256]{1,0:T(8,128)} %get-tuple-element.25) | copy-start | bytes 2359300
  473.8 33.3 %copy-start.16 = (f32[768,256]{1,0:T(8,128)S(1)}, f32[768,256]{1,0:T(8,128)}, u32[]{:S(2)}) copy-start(f32[768,256]{1,0:T(8,128)} %get-tuple-element.26) | copy-start | bytes 2359300
  473.8 143.9 %all-gather.12.cloned.1.call-start = ((), (), s32[]{:S(2)}) async-start(), calls=%async_computation.10 | async-start | bytes 2228224 | tf_op jit(solution)/shard_map/all_gather | solution.py:236
  507.0 7.8 %copy-start.21 = (bf16[768,256]{1,0:T(8,128)(2,1)S(1)}, bf16[768,256]{1,0:T(8,128)(2,1)}, u32[]{:S(2)}) copy-start(bf16[768,256]{1,0:T(8,128)(2,1)} %reduce-scatter.8.cloned.1.call-done) | copy-start | bytes 1179652
  514.8 7.0 %copy-start.5 = (f32[768,1,256]{2,0,1:T(8,128)}, f32[768,1,256]{2,0,1:T(8,128)S(1)}, u32[]{:S(2)}) copy-start(f32[768,1,256]{2,0,1:T(8,128)S(1)} %get-tuple-element.31) | copy-start | bytes 2359300
  514.8 7.0 %copy-start.7 = (f32[768,1,256]{2,0,1:T(8,128)}, f32[768,1,256]{2,0,1:T(8,128)S(1)}, u32[]{:S(2)}) copy-start(f32[768,1,256]{2,0,1:T(8,128)S(1)} %get-tuple-element.32) | copy-start | bytes 2359300
  521.8 0.9 copy-start.9
  521.8 1.1 copy-start.11
  543.9 2.6 collective-permute-start
  546.6 3.2 collective-permute-start.1
  549.7 3.8 collective-permute-start.2
  553.5 4.4 collective-permute-start.3
  557.9 4.4 collective-permute-start.4
  562.3 4.4 collective-permute-start.5
  566.7 4.4 collective-permute-start.6
  571.9 59.1 %copy-start.6 = (f32[768,1,256]{2,0,1:T(8,128)S(1)}, f32[768,1,256]{2,0,1:T(8,128)}, u32[]{:S(2)}) copy-start(f32[768,1,256]{2,0,1:T(8,128)} %copy-done.5) | copy-start | bytes 2359300
  571.9 59.1 %copy-start.8 = (f32[768,1,256]{2,0,1:T(8,128)S(1)}, f32[768,1,256]{2,0,1:T(8,128)}, u32[]{:S(2)}) copy-start(f32[768,1,256]{2,0,1:T(8,128)} %copy-done.7) | copy-start | bytes 2359300
  571.9 59.1 %copy-start.10 = (f32[768,1,256]{2,0,1:T(8,128)S(1)}, f32[768,1,256]{2,0,1:T(8,128)}, u32[]{:S(2)}) copy-start(f32[768,1,256]{2,0,1:T(8,128)} %copy-done.9) | copy-start | bytes 2359300
  571.9 59.1 %copy-start.12 = (f32[768,1,256]{2,0,1:T(8,128)S(1)}, f32[768,1,256]{2,0,1:T(8,128)}, u32[]{:S(2)}) copy-start(f32[768,1,256]{2,0,1:T(8,128)} %copy-done.11) | copy-start | bytes 2359300
  622.0 22.3 %all-to-all-start = ((bf16[256,2,393]{2,1,0:T(2,128)(2,1)}), bf16[256,2,393]{2,1,0:T(2,128)(2,1)}, u32[]{:S(2)}, u32[]{:S(2)}) async-start(bf16[256,2,393]{2,1,0:T(2,128)(2,1)} %copy.226), calls=%async_computation.3 | async-start | bytes 1048576 | tf_op jit(solution)/shard_map/all_to_all | solution.py:241
  631.4 18.8 %copy-start.1 = (bf16[48,128,2,128]{3,2,1,0:T(2,128)(2,1)S(1)}, bf16[48,128,2,128]{3,2,1,0:T(2,128)(2,1)}, u32[]{:S(2)}) copy-start(bf16[48,128,2,128]{3,2,1,0:T(2,128)(2,1)} %param.27) | copy-start | bytes 9437188
Sparse Core Ops, SparseCore 0:
  33.0 33.4 all-gather.5
  80.1 61.6 all-gather.7
  248.8 90.8 reduce-scatter.3
  344.4 45.4 reduce-scatter.5
  427.2 31.3 all-gather.9
  473.9 33.0 reduce-scatter.7
  572.0 45.6 all-gather.11
